TPU v7x, 512 devices: a whole 4x8x8 slice. The times are simulated.
512 devices in a mesh: band: 32 (over z_hi, x, core), chan: 16 (over y, z_lo).
Axes of the slice: x: 4, y: 8, z: 8 (z_hi: 4, z_lo: 2; z = z_hi * 2 + z_lo), core: 2. Of those that a mesh axis runs over, the one named last changes fastest.
Arguments:
- image: bfloat16 [512, 128, 512], P('chan', 'band'), may hold values from -6 to 6
- filters: bfloat16 [9, 512, 512], P(None, None, 'chan'), may hold values from -0.09375 to 0.09375
- bias: bfloat16 [512], P('chan'), may hold values from -3 to 3
- upstream: bfloat16 [512, 128, 512], P('chan', 'band'), may hold values from -6 to 6
Outputs:
- features: bfloat16 [512, 128, 512], P('chan', 'band')
- image_grad: bfloat16 [512, 128, 512], P('chan', 'band')
All inputs are finite; a program needn't handle non-finite values.
Results may differ from a plain program's by a relative error of at most 0.001.
Values may be sent and summed in bfloat16 or wider, within the bound.
A program may use at most 64 MiB of HBM per device.

v0:
```python
import jax
import jax.numpy as jnp
from jax import lax
from jax.sharding import PartitionSpec as P


def with_halo(value, sides, width):
    for axis, dim in sides:
        size, length = (lax.axis_size(axis), value.shape[dim])
        up = [(i, (i + 1) % size) for i in range(size - 1)]
        down = [(j, i) for i, j in up]
        last = lax.slice_in_dim(value, length - width, length, axis=dim)
        first = lax.slice_in_dim(value, 0, width, axis=dim)
        before = lax.ppermute(last, axis, up)
        after = lax.ppermute(first, axis, down)
        value = jnp.concatenate([before, value, after], axis=dim)
    return value


def tap_forward(weights, source, row_count, col_count):
    result = None
    for tap_row in range(3):
        for tap_col in range(3):
            term = jnp.einsum(
                "oi,irc->orc",
                weights[tap_row * 3 + tap_col],
                source[:, tap_row : tap_row + row_count, tap_col : tap_col + col_count],
                preferred_element_type=jnp.float32,
            )
            result = term if result is None else result + term
    return result


def tap_backward(weights, source, row_count, col_count):
    result = None
    for tap_row in range(3):
        for tap_col in range(3):
            term = jnp.einsum(
                "oi,orc->irc",
                weights[tap_row * 3 + tap_col],
                source[
                    :, 2 - tap_row : 2 - tap_row + row_count, 2 - tap_col : 2 - tap_col + col_count
                ],
                preferred_element_type=jnp.float32,
            )
            result = term if result is None else result + term
    return result


def per_device(image, filters, bias, upstream):
    row_count = image.shape[1]
    col_count = image.shape[2]
    stacked = jnp.stack([image, upstream])
    with_rims = with_halo(stacked, (("band", 2),), 1)
    padded = jnp.pad(with_rims, ((0, 0), (0, 0), (0, 0), (1, 1)))
    outward = lax.all_to_all(filters, "chan", split_axis=1, concat_axis=2, tiled=True)
    w_part = outward
    forward_sum = tap_forward(
        w_part, lax.all_gather(padded[0], "chan", axis=0, tiled=True), row_count, col_count
    )
    w_part = filters
    grad_sum = tap_backward(
        w_part, lax.all_gather(padded[1], "chan", axis=0, tiled=True), row_count, col_count
    )
    features = (forward_sum + bias.astype(jnp.float32)[:, None, None]).astype(jnp.bfloat16)
    image_grad = grad_sum.astype(jnp.bfloat16)
    return (features, image_grad)


def solution(mesh):
    return jax.shard_map(
        per_device,
        mesh=mesh,
        in_specs=(
            P("chan", "band", None),
            P(None, None, "chan"),
            P("chan"),
            P("chan", "band", None),
        ),
        out_specs=(P("chan", "band", None), P("chan", "band", None)),
        check_vma=False,
    )
```

profile of v0, /device:TPU:18, one launch (start us, length us, event | category | flops | bytes accessed | tf_op | source)
XLA Modules:
  0.0 245.0 jit_solution(1787459723346832427)
XLA Ops:
  7.2 0.0 all-gather.7.cloned.1.call-start
  7.2 1.0 copy_bitcast_fusion.1
  8.3 1.9 collective-permute-start.1
  10.2 2.4 collective-permute-start
  12.6 3.2 %collective-permute-done = bf16[2,32,1,512]{3,1,2,0:T(8,128)(2,1)S(1)} collective-permute-done((bf16[2,32,1,512]{3,1,2,0:T(8,128)(2,1)S(1)}, bf16[2,32,1,512]{3,1,2,0:T(8,128)(2,1)S(1)}, u32[]{:S(2)}, u32[]{:S(2)}) %collective-permute-start) | collective-permute-done | bytes 65568 | tf_op jit(solution)/shard_map/ppermute | solution.py:14
  15.8 0.3 select_maximum_fusion
  16.1 0.9 fusion.122
  17.0 0.0 all-gather.5.cloned.1.call-start
  17.0 0.7 all-gather.5.cloned.1.call-update
  17.7 2.0 copy.13
  19.7 2.0 reshape.52
  21.7 9.3 %all-to-all-start = ((bf16[16,2,4608]{2,1,0:T(2,128)(2,1)}), bf16[16,2,4608]{2,1,0:T(2,128)(2,1)S(1)}, u32[]{:S(2)}, u32[]{:S(2)}) async-start(bf16[16,2,4608]{2,1,0:T(2,128)(2,1)} %reshape.52), calls=%async_computation | async-start | bytes 589824 | tf_op jit(solution)/shard_map/all_to_all | solution.py:56
  31.0 10.4 %all-to-all-done = bf16[16,2,4608]{2,1,0:T(2,128)(2,1)S(1)} async-done(((bf16[16,2,4608]{2,1,0:T(2,128)(2,1)}), bf16[16,2,4608]{2,1,0:T(2,128)(2,1)S(1)}, u32[]{:S(2)}, u32[]{:S(2)}) %all-to-all-start) | async-done | bytes 294944 | tf_op jit(solution)/shard_map/all_to_all | solution.py:56
  41.4 1.4 reshape.53
  42.7 0.8 copy.20
  43.6 0.2 fusion.121
  43.8 0.2 reshape.33
  44.0 0.2 reshape.32
  44.1 0.2 reshape.31
  44.3 0.2 reshape.30
  44.4 0.2 reshape.29
  44.6 0.2 reshape.28
  44.8 0.2 reshape.27
  44.9 0.2 reshape.26
  45.1 0.2 reshape.25
  45.2 76.4 %all-gather.7.cloned.1.call-done = bf16[1,512,6,514]{3,1,2,0:T(8,128)(2,1)} async-done(((bf16[1,32,6,514]{3,1,2,0:T(8,128)(2,1)}), bf16[1,512,6,514]{3,1,2,0:T(8,128)(2,1)}) %all-gather.7.cloned.1.call-update) | async-done | bytes 3158032 | tf_op jit(solution)/shard_map/all_gather | solution.py:63
  121.6 2.2 fusion
  123.8 2.5 %fusion.2 = f32[4,512,32]{1,2,0:T(8,128)S(1)} fusion(bf16[512,6,514]{2,0,1:T(8,128)(2,1)} %bitcast.80, bf16[9,512,32]{1,2,0:T(8,128)(2,1)S(1)} %copy-done.3), kind=kOutput, calls=%fused_computation.2 | convolution fusion | flops 67108864 | bytes 2392064 | tf_op jit(solution)/shard_map/oi,orc->irc/dot_general | solution.py:38
  126.4 0.8 fusion.4
  127.1 0.5 fusion.6
  127.6 0.8 fusion.8
  128.4 0.8 fusion.10
  129.2 0.5 fusion.12
  129.6 0.8 fusion.14
  130.4 94.7 %all-gather.5.cloned.1.call-done = bf16[1,512,6,514]{3,1,2,0:T(8,128)(2,1)} async-done(((bf16[1,32,6,514]{3,1,2,0:T(8,128)(2,1)}), bf16[1,512,6,514]{3,1,2,0:T(8,128)(2,1)}) %all-gather.5.cloned.1.call-update) | async-done | bytes 3158032 | tf_op jit(solution)/shard_map/all_gather | solution.py:59
  225.1 2.7 %fusion.18 = f32[4,512,32]{1,2,0:T(8,128)S(1)} fusion(bf16[32,512,1]{1,0,2:T(8,128)(2,1)S(1)} %reshape.33, bf16[512,6,514]{2,0,1:T(8,128)(2,1)} %bitcast.88), kind=kOutput, calls=%fused_computation.18 | convolution fusion | flops 67108864 | bytes 2392064 | tf_op jit(solution)/shard_map/oi,irc->orc/dot_general | solution.py:24
  227.8 2.5 %fusion.20 = f32[4,512,32]{1,2,0:T(8,128)S(1)} fusion(bf16[32,512,1]{1,0,2:T(8,128)(2,1)S(1)} %reshape.32, bf16[512,6,514]{2,0,1:T(8,128)(2,1)} %bitcast.89), kind=kOutput, calls=%fused_computation.20 | convolution fusion | flops 67108864 | bytes 2392064 | tf_op jit(solution)/shard_map/oi,irc->orc/dot_general | solution.py:24
  230.3 0.5 fusion.22
  230.8 0.8 fusion.24
  231.6 0.8 fusion.26
  232.4 0.5 fusion.28
  232.8 0.8 fusion.30
  233.6 0.8 fusion.32
  234.4 0.5 fusion.93
  235.0 0.8 copy.15
  235.7 0.9 copy-done.1
  236.6 0.8 fusion.96
  237.4 0.8 copy.16
  (13 shorter events, 0.1 us)
Async XLA Ops:
  7.2 10.6 %copy-start.3 = (bf16[9,512,32]{1,2,0:T(8,128)(2,1)S(1)}, bf16[9,512,32]{1,2,0:T(8,128)(2,1)}, u32[]{:S(2)}) copy-start(bf16[9,512,32]{1,2,0:T(8,128)(2,1)} %param.5) | copy-start | bytes 884740
  7.2 114.4 %all-gather.7.cloned.1.call-start = ((), (), s32[]{:S(2)}) async-start(), calls=%async_computation.2 | async-start | bytes 4177920 | tf_op jit(solution)/shard_map/all_gather | solution.py:63
  8.3 4.3 %collective-permute-start.1 = (bf16[2,32,1,512]{3,1,2,0:T(8,128)(2,1)S(1)}, bf16[2,32,1,512]{3,1,2,0:T(8,128)(2,1)S(1)}, u32[]{:S(2)}, u32[]{:S(2)}) collective-permute-start(bf16[2,32,1,512]{3,1,2,0:T(8,128)(2,1)S(1)} %get-tuple-element.18), channel_id=1, source_target_pairs={{16,0},{32,16},{48,32},{64,48},{80,64},{96,80},{112,96},{128,112},... | collective-permute-start | bytes 196616 | tf_op jit(solution)/shard_map/ppermute | solution.py:15
  10.2 5.6 %collective-permute-start = (bf16[2,32,1,512]{3,1,2,0:T(8,128)(2,1)S(1)}, bf16[2,32,1,512]{3,1,2,0:T(8,128)(2,1)S(1)}, u32[]{:S(2)}, u32[]{:S(2)}) collective-permute-start(bf16[2,32,1,512]{3,1,2,0:T(8,128)(2,1)S(1)} %get-tuple-element.17), channel_id=1, source_target_pairs={{0,16},{16,32},{32,48},{48,64},{64,80},{80,96},{96,112},{112,128},... | collective-permute-start | bytes 196616 | tf_op jit(solution)/shard_map/ppermute | solution.py:14
  17.0 208.1 %all-gather.5.cloned.1.call-start = ((), (), s32[]{:S(2)}) async-start(), calls=%async_computation.1 | async-start | bytes 4177920 | tf_op jit(solution)/shard_map/all_gather | solution.py:59
  17.7 13.2 %copy-start.4 = (bf16[32]{0:T(256)(128)(2,1)S(1)}, bf16[32]{0:T(256)(128)(2,1)}, u32[]{:S(2)}) copy-start(bf16[32]{0:T(256)(128)(2,1)} %param.6) | copy-start | bytes 196
  21.7 19.7 %all-to-all-start = ((bf16[16,2,4608]{2,1,0:T(2,128)(2,1)}), bf16[16,2,4608]{2,1,0:T(2,128)(2,1)S(1)}, u32[]{:S(2)}, u32[]{:S(2)}) async-start(bf16[16,2,4608]{2,1,0:T(2,128)(2,1)} %reshape.52), calls=%async_computation | async-start | bytes 589824 | tf_op jit(solution)/shard_map/all_to_all | solution.py:56
  121.6 4.7 %copy-start = (bf16[1,512,6,514]{3,1,2,0:T(8,128)(2,1)S(1)}, bf16[1,512,6,514]{3,1,2,0:T(8,128)(2,1)}, u32[]{:S(2)}) copy-start(bf16[1,512,6,514]{3,1,2,0:T(8,128)(2,1)} %all-gather.7.cloned.1.call-done) | copy-start | bytes 9474052
  225.1 5.2 %copy-start.2 = (bf16[1,512,6,514]{3,1,2,0:T(8,128)(2,1)S(1)}, bf16[1,512,6,514]{3,1,2,0:T(8,128)(2,1)}, u32[]{:S(2)}) copy-start(bf16[1,512,6,514]{3,1,2,0:T(8,128)(2,1)} %all-gather.5.cloned.1.call-done) | copy-start | bytes 9474052
  234.4 2.2 copy-start.1
Sparse Core Ops, SparseCore 0:
  17.1 104.4 all-gather.6
  123.7 101.3 all-gather.4
where the time goes:
time: 245 us
  waiting for transfers between devices  185 us (76%)
  matrix products  19.4 us (8%)
  between operations  14.2 us (6%)
  starting transfers between devices  13.7 us (6%)
  local copies, waits for them, and re-layouts  12.1 us (5%)
    all_gather x1, waiting for transfers between devices, per_device(): lax.all_gather(padded[0], 'chan', axis=0, tiled=True)  94.7 us
    all_gather x1, waiting for transfers between devices, per_device(): lax.all_gather(padded[1], 'chan', axis=0, tiled=True)  76.4 us
    all_to_all x1, waiting for transfers between devices, per_device(): lax.all_to_all(filters, 'chan', split_axis=1, concat_axis=2, tiled=True)  10.4 us
    dot_general x9, matrix products, tap_forward(): jnp.einsum('oi,irc->orc', weights[tap_row * 3 + tap_col], source[:, tap_r...  9.83 us
    dot_general x9, matrix products, tap_backward(): jnp.einsum('oi,orc->irc', weights[tap_row * 3 + tap_col], source[:, 2 - t...  9.61 us
    all_to_all x1, starting transfers between devices, per_device(): lax.all_to_all(filters, 'chan', split_axis=1, concat_axis=2, tiled=True)  9.26 us
    unnamed x15, local copies, waits for them, and re-layouts  7.71 us
  transfers between devices with their start and end apart: 5, of which 4 were waited for; matrix products, arithmetic and copies ran while one was open for 7% of the time, Pallas kernels for 0%

commit v1 on v0

v1 whole, which is shorter than its diff:
```python
import jax
import jax.numpy as jnp
from jax import lax
from jax.experimental import pallas as pl
from jax.experimental.pallas import tpu as pltpu
from jax.sharding import PartitionSpec as P

MESH = pl.DeviceIdType.MESH
BF16, F32 = jnp.bfloat16, jnp.float32


def kernel(keep, give, filt, bias, mine, other, gathered, weights, packed, pieces,
           products, rim_out, rim_in, bias_in, staged,
           ring_send, ring_recv, pair_send, pair_recv, piece_send, piece_recv,
           share_send, rim_send, rim_recv, out_send, out_recv):
    band, chan = lax.axis_index("band"), lax.axis_index("chan")
    core, x, z_hi = band % 2, (band // 2) % 4, band // 8
    y, z_lo = chan // 2, chan % 2
    partner = {"band": band, "chan": chan + 1 - 2 * z_lo}
    up_ring = {"band": band, "chan": (chan + 2) % 16}
    down_ring = {"band": band, "chan": (chan + 14) % 16}
    above = {"band": (band + 31) % 32, "chan": chan}
    below = {"band": (band + 1) % 32, "chan": chan}

    def same_place(k):
        other_x, other_core = (x + k // 2) % 4, (core + k % 2) % 2
        return {"band": z_hi * 8 + other_x * 2 + other_core, "chan": chan}

    def same_band(k):
        return {"band": band, "chan": (chan + k) % 16}

    barrier = pltpu.get_barrier_semaphore()
    peers = [same_band(k) for k in range(1, 16)] + [same_place(k) for k in range(1, 8)]
    for peer in peers + [above, below]:
        pl.semaphore_signal(barrier, inc=1, device_id=peer, device_id_type=MESH)
    pl.semaphore_wait(barrier, len(peers) + 2)

    def remote(src, dst, send, recv, where):
        return pltpu.make_async_remote_copy(
            src_ref=src, dst_ref=dst, send_sem=send, recv_sem=recv,
            device_id=where, device_id_type=MESH)

    partner_chan = chan + 1 - 2 * z_lo
    started = []

    def ring(direction, hop, src, owner):
        copy = remote(src, gathered.at[:, owner], ring_send.at[direction, hop],
                      ring_recv.at[direction, hop], up_ring if direction == 0 else down_ring)
        copy.start()
        started.append(copy)

    pair = remote(give, gathered.at[:, chan], pair_send.at[0], pair_recv.at[0], partner)
    pair.start()
    ring(0, 0, keep, chan)
    ring(1, 0, keep, chan)
    biases = remote(bias, bias_in, pair_send.at[1], pair_recv.at[1], partner)
    biases.start()

    @pl.when((core == z_lo) & (x == y % 4))
    def _():
        lane = lax.broadcasted_iota(jnp.int32, (32, 128), 1)
        for q in range(4):
            for j in range(5):
                a = filt[2 * j, :, 128 * q : 128 * q + 128].astype(F32)
                b = filt[2 * j + 1, :, 128 * q : 128 * q + 128].astype(F32) if j < 4 else a
                packed[2 * q, j] = jnp.where(lane < 64, a, pltpu.roll(b, 64, 1)).astype(BF16)
                packed[2 * q + 1, j] = jnp.where(lane < 64, pltpu.roll(a, 64, 1), b).astype(BF16)
        for d in range(1, 8):
            remote(packed.at[(y + d) % 8], pieces.at[:, chan], piece_send.at[d],
                   piece_recv.at[chan], {"band": band, "chan": 2 * ((y + d) % 8)}).start()

        @pl.when(z_lo == 0)
        def _():
            pltpu.make_async_copy(packed.at[y], pieces.at[:, chan], piece_recv.at[chan]).start()

        @pl.when(z_lo == 1)
        def _():
            remote(packed.at[y], pieces.at[:, chan], piece_send.at[0],
                   piece_recv.at[chan], partner).start()

    gradient_filters = remote(filt, weights.at[0:9, 0:32], pair_send.at[2], pair_recv.at[2], partner)

    @pl.when(z_lo == 0)
    def _():
        gradient_filters.start()

    @pl.when(z_lo == 1)
    def _():
        weights[0:9, 32:64] = filt[...]

    gathered[:, chan] = keep[...]

    def piece_wait(owner):
        remote(packed.at[0], pieces.at[:, owner], piece_send.at[0], piece_recv.at[owner], partner).wait_recv()

    def ring_wait(direction, hop, owner):
        remote(keep, gathered.at[:, owner], ring_send.at[direction, hop],
               ring_recv.at[direction, hop], partner).wait_recv()

    pair.wait_recv()
    ring(0, 1, gathered.at[:, partner_chan], partner_chan)
    ring(1, 1, gathered.at[:, partner_chan], partner_chan)

    def owner_of(direction, hop):
        away = hop // 2 + 1
        base = (chan + 16 - 2 * away) % 16 if direction == 0 else (chan + 2 * away) % 16
        if hop == 6:
            return base if direction == 0 else base + 1 - 2 * z_lo
        return base if hop % 2 == 0 else base + 1 - 2 * z_lo

    for hop in range(7):
        for direction in range(2):
            owner = owner_of(direction, hop)
            ring_wait(direction, hop, owner)
            if hop + 2 < 6 or (hop + 2 == 6 and direction == 0):
                ring(direction, hop + 2, gathered.at[:, owner], owner)
            if hop == 5 and direction == 1:
                ring(1, 6, gathered.at[:, owner], owner)
        if hop == 1:
            @pl.when(z_lo == 0)
            def _():
                for m in range(2):
                    owner = 2 * (x + 4 * m) + core
                    piece_wait(owner)
                    for k in range(1, 8):
                        remote(pieces.at[:, owner], pieces.at[:, owner], share_send.at[m, k],
                               piece_recv.at[owner], same_place(k)).start()
        if hop == 4:
            @pl.when(z_lo == 0)
            def _():
                for k in range(1, 8):
                    band_of = same_place(k)["band"]
                    for m in range(2):
                        piece_wait(2 * ((band_of // 2) % 4 + 4 * m) + band_of % 2)
                for j in range(5):
                    weights[2 * j : 2 * j + 2] = pieces[j].reshape(512, 128).T.reshape(2, 64, 512)

            @pl.when(z_lo == 1)
            def _():
                gradient_filters.wait_recv()

    lhs = weights[0:9].reshape(576, 512)

    def multiply(q, carry):
        for half in range(2):
            columns = slice(256 * half, 256 * half + 256)
            rhs = gathered[q, :, :, columns].reshape(512, 256)
            products[q, :, :, columns] = jnp.dot(
                lhs, rhs, preferred_element_type=F32).reshape(9, 64, 256)
        return carry

    lax.fori_loop(0, 4, multiply, 0)

    column = lax.broadcasted_iota(jnp.int32, (64, 512), 1)

    def tap(a, b):
        return 3 * a + b + z_lo * (8 - 2 * (3 * a + b))

    def row_sum(terms):
        left, mid, right = [sum(products[q, tap(a, b)] for q, a in terms) for b in range(3)]
        left = jnp.where(column == 0, 0.0, pltpu.roll(left, 1, 1))
        right = jnp.where(column == 511, 0.0, pltpu.roll(right, 511, 1))
        return left + mid + right

    rim_out[0] = row_sum([(0, 2)])
    to_above = remote(rim_out.at[0], rim_in.at[0], rim_send.at[0], rim_recv.at[0], above)
    to_above.start()
    rim_out[1] = row_sum([(3, 0)])
    to_below = remote(rim_out.at[1], rim_in.at[1], rim_send.at[1], rim_recv.at[1], below)
    to_below.start()

    biases.wait_recv()
    own_bias, partner_bias = bias[:, 0:1], bias_in[:, 0:1]
    offset = jnp.concatenate([own_bias, partner_bias], axis=0)
    offset = jnp.where(z_lo == 0, offset, jnp.zeros_like(offset))
    outgoing = []
    for r in (1, 2, 0, 3):
        total = row_sum([(r + a - 1, a) for a in range(3) if 0 <= r + a - 1 < 4])
        if r == 0:
            to_below.wait_recv()
            total = total + jnp.where(band > 0, rim_in[1], 0.0)
        if r == 3:
            to_above.wait_recv()
            total = total + jnp.where(band < 31, rim_in[0], 0.0)
        total = (total + offset).astype(BF16)
        low, high = total[0:32], total[32:64]
        mine[r] = jnp.where(z_lo == 0, low, high)
        staged[r] = jnp.where(z_lo == 0, high, low)
        copy = remote(staged.at[r], other.at[r], out_send.at[r], out_recv.at[r], partner)
        copy.start()
        outgoing.append(copy)

    for copy in started:
        copy.wait_send()
    pair.wait_send()
    biases.wait_send()
    to_above.wait_send()
    to_below.wait_send()

    @pl.when((core == z_lo) & (x == y % 4))
    def _():
        for d in range(1, 8):
            remote(packed.at[0], pieces.at[:, 0], piece_send.at[d], piece_recv.at[0], partner).wait_send()

        @pl.when(z_lo == 1)
        def _():
            remote(packed.at[0], pieces.at[:, 0], piece_send.at[0], piece_recv.at[0], partner).wait_send()

    @pl.when(z_lo == 0)
    def _():
        gradient_filters.wait_send()
        for m in range(2):
            for k in range(1, 8):
                remote(pieces.at[:, 0], pieces.at[:, 0], share_send.at[m, k], piece_recv.at[0], partner).wait_send()

    for copy in outgoing:
        copy.wait()


def per_device(image, filters, bias, upstream):
    forward = lax.axis_index("chan") % 2 == 0
    rows_first = [jnp.transpose(value, (1, 0, 2)) for value in (image, upstream)]
    keep = jnp.where(forward, *rows_first)
    give = jnp.where(forward, *rows_first[::-1])
    filt = jnp.transpose(filters, (0, 2, 1))
    wide_bias = jnp.broadcast_to(bias.astype(F32)[:, None], (32, 128))
    block = jax.ShapeDtypeStruct((4, 32, 512), BF16)
    vmem = pl.BlockSpec(memory_space=pltpu.VMEM)
    dma = pltpu.SemaphoreType.DMA
    mine, other = pl.pallas_call(
        kernel,
        out_shape=(block, block),
        in_specs=[vmem] * 4,
        out_specs=(vmem, vmem),
        scratch_shapes=[
            pltpu.VMEM((4, 16, 32, 512), BF16),
            pltpu.VMEM((10, 64, 512), BF16),
            pltpu.VMEM((8, 5, 32, 128), BF16),
            pltpu.VMEM((5, 16, 32, 128), BF16),
            pltpu.VMEM((4, 9, 64, 512), F32),
            pltpu.VMEM((2, 64, 512), F32),
            pltpu.VMEM((2, 64, 512), F32),
            pltpu.VMEM((32, 128), F32),
            pltpu.VMEM((4, 32, 512), BF16),
            dma((2, 7)), dma((2, 7)), dma((3,)), dma((3,)), dma((8,)), dma((16,)),
            dma((2, 8)), dma((2,)), dma((2,)), dma((4,)), dma((4,)),
        ],
        compiler_params=pltpu.CompilerParams(
            collective_id=0, has_side_effects=True, vmem_limit_bytes=40 << 20),
        name="conv_both",
    )(keep, give, filt, wide_bias)
    features = jnp.transpose(jnp.where(forward, mine, other), (1, 0, 2))
    image_grad = jnp.transpose(jnp.where(forward, other, mine), (1, 0, 2))
    return features, image_grad


def solution(mesh):
    return jax.shard_map(
        per_device,
        mesh=mesh,
        in_specs=(
            P("chan", "band", None),
            P(None, None, "chan"),
            P("chan"),
            P("chan", "band", None),
        ),
        out_specs=(P("chan", "band", None), P("chan", "band", None)),
        check_vma=False,
    )
```

time: 245 us -> 52.5 us (0.21)
  the two profiles are of different devices: /device:TPU:18 before, /device:TPU:8 now
where the time goes in v1:
time: 52.5 us; the launch traced here: 52.4 us
  Pallas kernels  48.4 us (92%)
  local copies, waits for them, and re-layouts  2.29 us (4%)
  other arithmetic  1.04 us (2%)
  between operations  0.68 us (1%)
    pallas_call x1, Pallas kernels, per_device(): pl.pallas_call(kernel, out_shape=(block, block), in_specs=[vmem] * 4, out...  48.4 us
    unnamed x4, local copies, waits for them, and re-layouts  1.52 us

profile of v1, /device:TPU:8, one launch (start us, length us, event | category | flops | bytes accessed | tf_op | source)
XLA Modules:
  0.0 52.4 jit_solution(2560366604337174146)
XLA Ops:
  0.6 0.0 copy-start
  0.7 0.8 %broadcast_in_dim.2.bias = f32[32,128]{1,0:T(8,128)S(1)} broadcast(bf16[32]{0:T(256)(128)(2,1)} %param.6), dimensions={0} | broadcast | bytes 16448 | tf_op jit(solution)/shard_map/broadcast_in_dim | solution.py:226
  1.4 1.0 %select_bitcast_fusion.2 = (bf16[4,32,512]{2,1,0:T(8,128)(2,1)S(1)}, bf16[4,32,512]{2,1,0:T(8,128)(2,1)S(1)}) fusion(pred[]{:T(512)S(6)} %eq.5, bf16[32,4,512]{2,1,0:T(4,128)(2,1)} %param.7, bf16[32,4,512]{2,1,0:T(4,128)(2,1)} %param.4), kind=kLoop, calls=%fused_computation.2 | loop fusion | flops 131072 | bytes 524289 | tf_op jit(solution)/shard_map/jit(_where)/select_n | solution.py:224
  2.4 0.0 copy-done
  2.5 48.4 %conv_both.1 = (bf16[4,32,512]{2,1,0:T(8,128)(2,1)S(1)}, bf16[4,32,512]{2,1,0:T(8,128)(2,1)S(1)}) custom-call(bf16[4,32,512]{2,1,0:T(8,128)(2,1)S(1)} %get-tuple-element.11.keep, bf16[4,32,512]{2,1,0:T(8,128)(2,1)S(1)} %get-tuple-element.10.give, bf16[9,32,512]{2,1,0:T(8,128)(2,1)S(1)} %bitcast.9, f32[32,128]{1,0:T(8,128)S(1)} %broadcast_in_dim.2.bias), custom_call_target="tpu_custom_call" | custom-call | tf_op jit(solution)/shard_map/conv_both/pallas_call | solution.py:230
  50.9 0.8 %copy.11 = bf16[32,4,512]{2,1,0:T(4,128)(2,1)} copy(bf16[32,4,512]{2,0,1:T(8,128)(2,1)S(1)} %get-tuple-element.8) | data formatting | bytes 262144
  51.6 0.8 %copy.10 = bf16[32,4,512]{2,1,0:T(4,128)(2,1)} copy(bf16[32,4,512]{2,0,1:T(8,128)(2,1)S(1)} %get-tuple-element.9) | data formatting | bytes 262144
  (1 shorter events, 0.0 us)
Async XLA Ops:
  0.6 1.8 %copy-start = (bf16[9,512,32]{1,2,0:T(8,128)(2,1)S(1)}, bf16[9,512,32]{1,2,0:T(8,128)(2,1)}, u32[]{:S(2)}) copy-start(bf16[9,512,32]{1,2,0:T(8,128)(2,1)} %param.5) | copy-start | bytes 884740

commit v2 on v1

v2 whole, which is shorter than its diff:
```python
import jax
import jax.numpy as jnp
from jax import lax
from jax.experimental import pallas as pl
from jax.experimental.pallas import tpu as pltpu
from jax.sharding import PartitionSpec as P

MESH = pl.DeviceIdType.MESH
BF16, F32 = jnp.bfloat16, jnp.float32


def kernel(keep, give, filt, bias, mine, other, gathered, halo, weights, packed, pieces,
           products, halo_products, bias_own, bias_in, staged,
           ring_send, ring_recv, pair_send, pair_recv, halo_send, halo_recv,
           filter_send, filter_recv, relay_send, piece_send, piece_recv, share_send,
           out_send, out_recv):
    band, chan = lax.axis_index("band"), lax.axis_index("chan")
    core, x, z_hi = band % 2, (band // 2) % 4, band // 8
    y, z_lo = chan // 2, chan % 2
    partner_chan = chan + 1 - 2 * z_lo
    partner = {"band": band, "chan": partner_chan}
    ring_next = ({"band": band, "chan": (chan + 2) % 16}, {"band": band, "chan": (chan + 14) % 16})
    twin = {"band": band + 1 - 2 * core, "chan": chan}
    outer_ok = ((core == 0) & (band > 0)) | ((core == 1) & (band < 31))
    outer = {"band": (band + 31 + 2 * core) % 32, "chan": chan}
    sends_filters = (core == z_lo) & (x == y % 4)

    def same_place(k):
        other_x, other_core = (x + k // 2) % 4, (core + k % 2) % 2
        return {"band": z_hi * 8 + other_x * 2 + other_core, "chan": chan}

    def slot_at(owner, place):
        return (owner + 16 - 4 * (((place + 7) // 2) % 4)) % 16

    def slot_of(owner):
        return slot_at(owner, y)

    def remote(src, dst, send, recv, where):
        return pltpu.make_async_remote_copy(
            src_ref=src, dst_ref=dst, send_sem=send, recv_sem=recv,
            device_id=where, device_id_type=MESH)

    barrier = pltpu.get_barrier_semaphore()

    def greet(where):
        pl.semaphore_signal(barrier, inc=1, device_id=where, device_id_type=MESH)

    for where in (partner, *ring_next):
        greet(where)

    @pl.when(outer_ok)
    def _():
        greet(outer)

    greet(twin)

    @pl.when(z_lo == 0)
    def _():
        for m in range(2):
            source = 2 * (x + 4 * m) + core

            @pl.when(source != chan)
            def _():
                greet({"band": band, "chan": source})
        for k in range(1, 8):
            if k != 1:
                greet(same_place(k))

    targets = 4 + jnp.where(outer_ok, 1, 0) + jnp.where(z_lo == 0, 6, 0)
    targets = targets + jnp.where(sends_filters, 7 + z_lo, 0)
    pl.semaphore_wait(barrier, targets)

    first_row = (3 * core, 1 - core)
    row_count = (1, 3)

    def rows(part):
        return pl.ds(first_row[part], row_count[part])

    def ring(direction, hop, part, owner, src):
        place = (y + 1) % 8 if direction == 0 else (y + 7) % 8
        return remote(src, gathered.at[rows(part), slot_at(owner, place)],
                      ring_send.at[direction, hop, part], ring_recv.at[direction, hop, part],
                      ring_next[direction])

    def own_block(part, owner):
        return gathered.at[rows(part), slot_of(owner)]

    def halo_copy(side, owner, src):
        slot = slot_of(owner)
        return remote(src, halo.at[side, slot], halo_send.at[side, slot],
                      halo_recv.at[side, slot], twin if side else outer)

    def send_halo(part, owner, block):
        if part == 0:
            @pl.when(outer_ok)
            def _():
                halo_copy(0, owner, block(3 * core)).start()
        else:
            halo_copy(1, owner, block(3 - 3 * core)).start()

    def in_gathered(owner):
        return lambda row: gathered.at[row, slot_of(owner)]

    def in_keep(row):
        return keep.at[row]

    started = []

    def start(copy):
        copy.start()
        started.append(copy)

    pairs = [remote(give.at[rows(part)], gathered.at[rows(part), slot_of(chan)],
                    pair_send.at[part], pair_recv.at[part], partner) for part in range(2)]
    for part in range(2):
        start(pairs[part])
        for direction in range(2):
            start(ring(direction, 0, part, chan, keep.at[rows(part)]))
        send_halo(part, chan, in_keep)

    @pl.when(sends_filters)
    def _():
        lane = lax.broadcasted_iota(jnp.int32, (32, 128), 1)
        for q in range(4):
            for j in range(5):
                a = filt[2 * j, :, 128 * q : 128 * q + 128].astype(F32)
                b = filt[2 * j + 1, :, 128 * q : 128 * q + 128].astype(F32) if j < 4 else a
                packed[2 * q, j] = jnp.where(lane < 64, a, pltpu.roll(b, 64, 1)).astype(BF16)
                packed[2 * q + 1, j] = jnp.where(lane < 64, pltpu.roll(a, 64, 1), b).astype(BF16)
        for d in range(1, 8):
            place = (y + d) % 8
            slot = slot_at(chan, place)
            remote(packed.at[place], pieces.at[:, slot], piece_send.at[d],
                   piece_recv.at[slot], {"band": band, "chan": 2 * place}).start()
        slot = slot_of(chan)

        @pl.when(z_lo == 0)
        def _():
            pltpu.make_async_copy(packed.at[y], pieces.at[:, slot], piece_recv.at[slot]).start()

        @pl.when(z_lo == 1)
        def _():
            remote(packed.at[y], pieces.at[:, slot], piece_send.at[0],
                   piece_recv.at[slot], partner).start()

    turn = ((y + 7) // 2) % 4

    def lanes(j):
        return pl.ds(pl.multiple_of(128 * ((j + turn) % 4), 128), 128)

    def from_partner(j):
        column = pl.ds(pl.multiple_of(128 * (2 * core + j), 128), 128)
        return remote(filt.at[:, :, lanes(2 * core + j)], weights.at[0:9, 0:32, column],
                      filter_send.at[j], filter_recv.at[2 * core + j], partner)

    def hand_on(j):
        column = pl.ds(pl.multiple_of(128 * (2 * core + j), 128), 128)
        return remote(weights.at[0:9, 0:32, column], weights.at[0:9, 0:32, column],
                      relay_send.at[j], filter_recv.at[2 * core + j], twin)

    def filters_wait(j, place):
        remote(filt.at[:, :, 0:128], weights.at[0:9, 0:32, 0:128],
               relay_send.at[j], filter_recv.at[2 * place + j], twin).wait_recv()

    diagonal = (lax.broadcasted_iota(jnp.int32, (32, 32), 0)
                == lax.broadcasted_iota(jnp.int32, (32, 32), 1))
    spread = jnp.where(diagonal, jnp.broadcast_to(bias[...].astype(F32), (32, 32)), 0.0)
    bias_own[...] = jnp.broadcast_to(jnp.sum(spread, axis=1, keepdims=True), (32, 128))
    biases = remote(bias_own, bias_in, pair_send.at[2], pair_recv.at[2], partner)
    start(biases)

    gathered[:, slot_of(chan)] = keep[...]

    @pl.when(z_lo == 1)
    def _():
        for j in range(4):
            weights[0:9, 32:64, 128 * j : 128 * j + 128] = filt[:, :, lanes(j)]

    for part in range(2):
        pairs[part].wait_recv()
        for direction in range(2):
            start(ring(direction, 1, part, partner_chan, own_block(part, partner_chan)))
        send_halo(part, partner_chan, in_gathered(partner_chan))

    @pl.when(z_lo == 0)
    def _():
        for j in range(2):
            from_partner(j).start()

    def piece_wait(owner):
        slot = slot_of(owner)
        remote(packed.at[0], pieces.at[:, slot], piece_send.at[0], piece_recv.at[slot], partner).wait_recv()

    def owner_of(direction, hop):
        away = hop // 2 + 1
        base = (chan + 16 - 2 * away) % 16 if direction == 0 else (chan + 2 * away) % 16
        swap = hop % 2 == 1 if hop < 6 else direction == 1
        return base + 1 - 2 * z_lo if swap else base

    def multiply(half):
        lhs = weights[0:9, :, 256 * half : 256 * half + 256].reshape(576, 256)

        def body(q, carry):
            for n in range(2):
                columns = slice(256 * n, 256 * n + 256)
                rhs = gathered[q, 8 * half : 8 * half + 8, :, columns].reshape(256, 256)
                result = jnp.dot(lhs, rhs, preferred_element_type=F32).reshape(9, 64, 256)
                if half:
                    result = products[q, :, :, columns] + result
                products[q, :, :, columns] = result
            return carry

        lax.fori_loop(0, 4, body, 0)

    def multiply_halo(side, half):
        turned = (core + z_lo + side) % 2
        lhs = weights[pl.ds(6 * turned, 3), :, 256 * half : 256 * half + 256].reshape(192, 256)
        rhs = halo[side, 8 * half : 8 * half + 8].reshape(256, 512)
        result = jnp.dot(lhs, rhs, preferred_element_type=F32).reshape(3, 64, 512)
        if half:
            result = halo_products[side] + result
        halo_products[side] = result

    def halo_wait(side, half):
        for slot in range(8 * half, 8 * half + 8):
            remote(keep.at[0], halo.at[side, slot], halo_send.at[side, slot],
                   halo_recv.at[side, slot], twin).wait_recv()

    for hop in range(7):
        for part in range(2):
            for direction in range(2):
                owner = owner_of(direction, hop)
                ring(direction, hop, part, owner, keep.at[rows(part)]).wait_recv()
                onward = hop + 2 if hop < 4 or (hop == 4 and direction == 0) else None
                if hop == 5 and direction == 1:
                    onward = 6
                if onward is not None:
                    start(ring(direction, onward, part, owner, own_block(part, owner)))
                send_halo(part, owner, in_gathered(owner))
        if hop == 1:
            @pl.when(z_lo == 0)
            def _():
                for m in range(2):
                    owner = 2 * (x + 4 * m) + core
                    piece_wait(owner)
                    slot = slot_of(owner)
                    for k in range(1, 8):
                        remote(pieces.at[:, slot], pieces.at[:, slot], share_send.at[m, k],
                               piece_recv.at[slot], same_place(k)).start()

            @pl.when(z_lo == 1)
            def _():
                for j in range(2):
                    filters_wait(j, core)
                    hand_on(j).start()
        if hop == 3:
            @pl.when(z_lo == 0)
            def _():
                for k in range(1, 8):
                    band_of = same_place(k)["band"]
                    for m in range(2):
                        piece_wait(2 * ((band_of // 2) % 4 + 4 * m) + band_of % 2)
                for j in range(5):
                    weights[2 * j : 2 * j + 2] = pieces[j].reshape(512, 128).T.reshape(2, 64, 512)

            @pl.when(z_lo == 1)
            def _():
                for j in range(2):
                    filters_wait(j, 1 - core)
        if hop == 4:
            multiply(0)
        if hop == 5:
            halo_wait(1, 0)
            multiply_halo(1, 0)

            @pl.when(outer_ok)
            def _():
                halo_wait(0, 0)
                multiply_halo(0, 0)

            biases.wait_recv()

    multiply(1)

    column = lax.broadcasted_iota(jnp.int32, (64, 512), 1)
    offset = jnp.concatenate([bias_own[:, 0:1], bias_in[:, 0:1]], axis=0)
    offset = jnp.where(z_lo == 0, offset, jnp.zeros_like(offset))

    def tap(a, b):
        return 3 * a + b + z_lo * (8 - 2 * (3 * a + b))

    def finish(r, terms, side=None):
        sums = [sum(products[q, tap(a, b)] for q, a in terms) for b in range(3)]
        if side is not None:
            sums = [s + halo_products[side, b + z_lo * (2 - 2 * b)] for b, s in enumerate(sums)]
        left, mid, right = sums
        left = jnp.where(column == 0, 0.0, pltpu.roll(left, 1, 1))
        right = jnp.where(column == 511, 0.0, pltpu.roll(right, 511, 1))
        total = (left + mid + right + offset).astype(BF16)
        low, high = total[0:32], total[32:64]
        mine[r] = jnp.where(z_lo == 0, low, high)
        staged[r] = jnp.where(z_lo == 0, high, low)
        copy = remote(staged.at[r], other.at[r], out_send.at[r], out_recv.at[r], partner)
        copy.start()
        return copy

    outgoing = [finish(r, [(r + a - 1, a) for a in range(3)]) for r in (1, 2)]
    halo_wait(1, 1)
    multiply_halo(1, 1)
    outgoing.append(finish(3 - 3 * core, [(3 - 3 * core, 1), (2 - core, 2 * core)], 1))

    @pl.when(outer_ok)
    def _():
        halo_wait(0, 1)
        multiply_halo(0, 1)

    @pl.when(jnp.logical_not(outer_ok))
    def _():
        halo_products[0] = jnp.zeros((3, 64, 512), F32)

    outgoing.append(finish(3 * core, [(3 * core, 1), (1 + core, 2 - 2 * core)], 0))

    for copy in started:
        copy.wait_send()
    for slot in range(16):
        remote(keep.at[0], halo.at[1, slot], halo_send.at[1, slot], halo_recv.at[1, slot], twin).wait_send()

    @pl.when(outer_ok)
    def _():
        for slot in range(16):
            remote(keep.at[0], halo.at[0, slot], halo_send.at[0, slot], halo_recv.at[0, slot], twin).wait_send()

    @pl.when(sends_filters)
    def _():
        for d in range(1, 8):
            remote(packed.at[0], pieces.at[:, 0], piece_send.at[d], piece_recv.at[0], partner).wait_send()

        @pl.when(z_lo == 1)
        def _():
            remote(packed.at[0], pieces.at[:, 0], piece_send.at[0], piece_recv.at[0], partner).wait_send()

    @pl.when(z_lo == 0)
    def _():
        for j in range(2):
            from_partner(j).wait_send()
        for m in range(2):
            for k in range(1, 8):
                remote(pieces.at[:, 0], pieces.at[:, 0], share_send.at[m, k], piece_recv.at[0], partner).wait_send()

    @pl.when(z_lo == 1)
    def _():
        for j in range(2):
            hand_on(j).wait_send()

    for copy in outgoing:
        copy.wait()


def per_device(image, filters, bias, upstream):
    forward = lax.axis_index("chan") % 2 == 0
    rows_first = [jnp.transpose(value, (1, 0, 2)) for value in (image, upstream)]
    keep = jnp.where(forward, *rows_first)
    give = jnp.where(forward, *rows_first[::-1])
    filt = jnp.transpose(filters, (0, 2, 1))
    block = jax.ShapeDtypeStruct((4, 32, 512), BF16)
    vmem = pl.BlockSpec(memory_space=pltpu.VMEM)
    dma = pltpu.SemaphoreType.DMA
    mine, other = pl.pallas_call(
        kernel,
        out_shape=(block, block),
        in_specs=[vmem] * 4,
        out_specs=(vmem, vmem),
        scratch_shapes=[
            pltpu.VMEM((4, 16, 32, 512), BF16),
            pltpu.VMEM((2, 16, 32, 512), BF16),
            pltpu.VMEM((10, 64, 512), BF16),
            pltpu.VMEM((8, 5, 32, 128), BF16),
            pltpu.VMEM((5, 16, 32, 128), BF16),
            pltpu.VMEM((4, 9, 64, 512), F32),
            pltpu.VMEM((2, 3, 64, 512), F32),
            pltpu.VMEM((32, 128), F32),
            pltpu.VMEM((32, 128), F32),
            pltpu.VMEM((4, 32, 512), BF16),
            dma((2, 7, 2)), dma((2, 7, 2)), dma((3,)), dma((3,)), dma((2, 16)), dma((2, 16)),
            dma((2,)), dma((4,)), dma((2,)), dma((8,)), dma((16,)), dma((2, 8)),
            dma((4,)), dma((4,)),
        ],
        compiler_params=pltpu.CompilerParams(
            collective_id=0, has_side_effects=True, vmem_limit_bytes=40 << 20),
        name="conv_both",
    )(keep, give, filt, bias.reshape(1, 32))
    mine, other = (jnp.transpose(value, (1, 0, 2)) for value in (mine, other))
    return jnp.where(forward, mine, other), jnp.where(forward, other, mine)


def solution(mesh):
    return jax.shard_map(
        per_device,
        mesh=mesh,
        in_specs=(
            P("chan", "band", None),
            P(None, None, "chan"),
            P("chan"),
            P("chan", "band", None),
        ),
        out_specs=(P("chan", "band", None), P("chan", "band", None)),
        check_vma=False,
    )
```

time: 52.5 us -> 45.8 us (0.87)
  the two profiles are of different devices: /device:TPU:8 before, /device:TPU:135 now
where the time goes in v2:
time: 45.8 us; the launch traced here: 45.7 us
  Pallas kernels  41.7 us (91%)
  local copies, waits for them, and re-layouts  2.16 us (5%)
  other arithmetic  1.09 us (2%)
  between operations  0.68 us (1%)
    pallas_call x1, Pallas kernels, per_device(): pl.pallas_call(kernel, out_shape=(block, block), in_specs=[vmem] * 4, out...  41.7 us
    unnamed x6, local copies, waits for them, and re-layouts  2.16 us
    select_n x1, other arithmetic, per_device(): give = jnp.where(forward, *rows_first[::-1])  1.06 us

profile of v2, /device:TPU:135, one launch (start us, length us, event | category | flops | bytes accessed | tf_op | source)
XLA Modules:
  0.0 45.7 jit_solution(2502062800265849465)
XLA Ops:
  0.6 0.0 copy-start
  0.7 1.1 %select_bitcast_fusion.2 = (bf16[4,32,512]{2,1,0:T(8,128)(2,1)S(1)}, bf16[4,32,512]{2,1,0:T(8,128)(2,1)S(1)}) fusion(pred[]{:T(512)S(6)} %eq.5, bf16[32,4,512]{2,1,0:T(4,128)(2,1)} %param.7, bf16[32,4,512]{2,1,0:T(4,128)(2,1)} %param.4), kind=kLoop, calls=%fused_computation.2 | loop fusion | flops 131072 | bytes 524289 | tf_op jit(solution)/shard_map/jit(_where)/select_n | solution.py:363
  1.7 0.0 copy-start.1
  1.7 0.0 copy-done
  1.7 0.6 %copy-done.1 = bf16[32]{0:T(256)(128)(2,1)S(1)} copy-done((bf16[32]{0:T(256)(128)(2,1)S(1)}, bf16[32]{0:T(256)(128)(2,1)}, u32[]{:S(2)}) %copy-start.1) | copy-done | bytes 88
  2.4 41.7 %conv_both.1 = (bf16[4,32,512]{2,1,0:T(8,128)(2,1)S(1)}, bf16[4,32,512]{2,1,0:T(8,128)(2,1)S(1)}) custom-call(bf16[4,32,512]{2,1,0:T(8,128)(2,1)S(1)} %get-tuple-element.11.keep, bf16[4,32,512]{2,1,0:T(8,128)(2,1)S(1)} %get-tuple-element.10.give, bf16[9,32,512]{2,1,0:T(8,128)(2,1)S(1)} %bitcast.10, bf16[1,32]{1,0:T(2,128)(2,1)S(1)} %bitcast.11), custom_call_target="tpu_custom_call" | custom-call | tf_op jit(solution)/shard_map/conv_both/pallas_call | solution.py:368
  44.2 0.8 %copy.11 = bf16[32,4,512]{2,1,0:T(4,128)(2,1)} copy(bf16[32,4,512]{2,0,1:T(8,128)(2,1)S(1)} %get-tuple-element.8) | data formatting | bytes 262144
  44.9 0.8 %copy.10 = bf16[32,4,512]{2,1,0:T(4,128)(2,1)} copy(bf16[32,4,512]{2,0,1:T(8,128)(2,1)S(1)} %get-tuple-element.9) | data formatting | bytes 262144
  (1 shorter events, 0.0 us)
Async XLA Ops:
  0.6 1.1 %copy-start = (bf16[9,512,32]{1,2,0:T(8,128)(2,1)S(1)}, bf16[9,512,32]{1,2,0:T(8,128)(2,1)}, u32[]{:S(2)}) copy-start(bf16[9,512,32]{1,2,0:T(8,128)(2,1)} %param.5) | copy-start | bytes 884740
  1.7 0.7 %copy-start.1 = (bf16[32]{0:T(256)(128)(2,1)S(1)}, bf16[32]{0:T(256)(128)(2,1)}, u32[]{:S(2)}) copy-start(bf16[32]{0:T(256)(128)(2,1)} %param.6) | copy-start | bytes 196

commit v3 on v2

v3 whole, which is shorter than its diff:
```python
import jax
import jax.numpy as jnp
from jax import lax
from jax.experimental import pallas as pl
from jax.experimental.pallas import tpu as pltpu
from jax.sharding import PartitionSpec as P

MESH = pl.DeviceIdType.MESH
BF16, F32 = jnp.bfloat16, jnp.float32


POSITION = (0, 2, 3, 1)


def kernel(image, upstream, filters, bias_row, features, image_grad, natural, give, filt, bias,
           gathered, halo, weights, packed, pieces, products, halo_products, bias_own, bias_in,
           staged, load_sem, ring_send, ring_recv, pair_send, pair_recv, halo_send, halo_recv,
           filter_send, filter_recv, relay_send, piece_send, piece_recv, share_send,
           out_send, out_recv):
    band, chan = lax.axis_index("band"), lax.axis_index("chan")
    core, x, z_hi = band % 2, (band // 2) % 4, band // 8
    y, z_lo = chan // 2, chan % 2
    partner_chan = chan + 1 - 2 * z_lo
    partner = {"band": band, "chan": partner_chan}
    ring_next = ({"band": band, "chan": (chan + 2) % 16}, {"band": band, "chan": (chan + 14) % 16})
    twin = {"band": band + 1 - 2 * core, "chan": chan}
    outer_ok = ((core == 0) & (band > 0)) | ((core == 1) & (band < 31))
    outer = {"band": (band + 31 + 2 * core) % 32, "chan": chan}
    sends_filters = (core == z_lo) & (x == y % 4)

    def slot_at(owner, place):
        return (owner + 16 - 4 * (((place + 7) // 2) % 4)) % 16

    def slot_of(owner):
        return slot_at(owner, y)

    def remote(src, dst, send, recv, where):
        return pltpu.make_async_remote_copy(
            src_ref=src, dst_ref=dst, send_sem=send, recv_sem=recv,
            device_id=where, device_id_type=MESH)

    loads = [pltpu.make_async_copy(filters, filt, load_sem.at[2]),
             pltpu.make_async_copy(bias_row, bias, load_sem.at[3])]
    keeping = [pltpu.make_async_copy(image, natural.at[z_lo], load_sem.at[0]),
               pltpu.make_async_copy(upstream, natural.at[1 - z_lo], load_sem.at[1])]
    for copy in keeping + loads:
        copy.start()

    barrier = pltpu.get_barrier_semaphore()

    def greet(where):
        pl.semaphore_signal(barrier, inc=1, device_id=where, device_id_type=MESH)

    def other_x(k):
        return {"band": z_hi * 8 + ((x + k) % 4) * 2 + core, "chan": chan}

    inner = (x == 1) | (x == 2)
    gives_filters, takes_filters = (z_lo == 0) & inner, (z_lo == 1) & inner

    def at_x(place, unit):
        return {"band": z_hi * 8 + place * 2 + unit, "chan": chan}

    for where in (partner, *ring_next, twin):
        greet(where)

    @pl.when(outer_ok)
    def _():
        greet(outer)

    @pl.when(z_lo == 0)
    def _():
        for m in range(2):
            source = 2 * (x + 4 * m) + core

            @pl.when(source != chan)
            def _():
                greet({"band": band, "chan": source})
        for k in range(1, 4):
            greet(other_x(k))

    @pl.when((z_lo == 1) & jnp.logical_not(inner))
    def _():
        for unit in range(2):
            greet(at_x(1 + x // 2, unit))

    own_slot = slot_of(chan)
    for copy in keeping:
        copy.wait()
    for row in range(4):
        gathered[POSITION[row], own_slot] = natural[0, :, row, :]
        give[POSITION[row]] = natural[1, :, row, :]

    targets = 4 + jnp.where(outer_ok, 1, 0) + jnp.where(z_lo == 0, 3, 0)
    targets = targets + jnp.where(sends_filters, 7 + z_lo, 0) + jnp.where(takes_filters, 2, 0)
    pl.semaphore_wait(barrier, targets)

    def rows(part):
        return slice(2 * part, 2 * part + 2)

    def ring(direction, hop, part, owner, src):
        place = (y + 1) % 8 if direction == 0 else (y + 7) % 8
        return remote(src, gathered.at[rows(part), slot_at(owner, place)],
                      ring_send.at[direction, hop, part], ring_recv.at[direction, hop, part],
                      ring_next[direction])

    def own_block(part, owner):
        return gathered.at[rows(part), slot_of(owner)]

    def halo_copy(side, owner, src):
        slot = slot_of(owner)
        return remote(src, halo.at[side, slot], halo_send.at[side, slot],
                      halo_recv.at[side, slot], twin if side else outer)

    def send_halo(owner):
        slot = slot_of(owner)

        @pl.when(outer_ok)
        def _():
            halo_copy(0, owner, gathered.at[core, slot]).start()

        halo_copy(1, owner, gathered.at[1 - core, slot]).start()

    started = []

    def start(copy):
        copy.start()
        started.append(copy)

    pairs = [remote(give.at[rows(part)], gathered.at[rows(part), own_slot],
                    pair_send.at[part], pair_recv.at[part], partner) for part in range(2)]
    for part in range(2):
        start(pairs[part])
        for direction in range(2):
            start(ring(direction, 0, part, chan, own_block(part, chan)))
    send_halo(chan)
    for copy in loads:
        copy.wait()

    @pl.when(sends_filters)
    def _():
        lane = lax.broadcasted_iota(jnp.int32, (32, 128), 1)
        for q in range(4):
            for j in range(5):
                a = filt[2 * j, :, 128 * q : 128 * q + 128].astype(F32)
                b = filt[2 * j + 1, :, 128 * q : 128 * q + 128].astype(F32) if j < 4 else a
                packed[2 * q, j] = jnp.where(lane < 64, a, pltpu.roll(b, 64, 1)).astype(BF16)
                packed[2 * q + 1, j] = jnp.where(lane < 64, pltpu.roll(a, 64, 1), b).astype(BF16)
        for d in range(1, 8):
            place = (y + d) % 8
            slot = slot_at(chan, place)
            remote(packed.at[place], pieces.at[:, slot], piece_send.at[d],
                   piece_recv.at[slot], {"band": band, "chan": 2 * place}).start()
        slot = slot_of(chan)

        @pl.when(z_lo == 0)
        def _():
            pltpu.make_async_copy(packed.at[y], pieces.at[:, slot], piece_recv.at[slot]).start()

        @pl.when(z_lo == 1)
        def _():
            remote(packed.at[y], pieces.at[:, slot], piece_send.at[0],
                   piece_recv.at[slot], partner).start()

    turn = ((y + 7) // 2) % 4

    def lanes(j):
        return pl.ds(pl.multiple_of(128 * ((j + turn) % 4), 128), 128)

    def from_partner(j):
        column = pl.ds(pl.multiple_of(128 * (2 * core + j), 128), 128)
        return remote(filt.at[:, :, lanes(2 * core + j)], weights.at[0:9, 0:32, column],
                      filter_send.at[j], filter_recv.at[2 * core + j], partner)

    def hand_on(j, k):
        column = pl.ds(pl.multiple_of(128 * (2 * core + j), 128), 128)
        place = jnp.where(x == 1, 0, 3)
        return remote(weights.at[0:9, 0:32, column], weights.at[0:9, 0:32, column],
                      relay_send.at[j, k], filter_recv.at[2 * core + j],
                      (twin, at_x(place, 0), at_x(place, 1))[k])

    def filters_wait(j, unit):
        remote(filt.at[:, :, 0:128], weights.at[0:9, 0:32, 0:128],
               relay_send.at[j, 0], filter_recv.at[2 * unit + j], twin).wait_recv()

    diagonal = (lax.broadcasted_iota(jnp.int32, (32, 32), 0)
                == lax.broadcasted_iota(jnp.int32, (32, 32), 1))
    spread = jnp.where(diagonal, jnp.broadcast_to(bias[...].astype(F32), (32, 32)), 0.0)
    bias_own[...] = jnp.broadcast_to(jnp.sum(spread, axis=1, keepdims=True), (32, 128))
    biases = remote(bias_own, bias_in, pair_send.at[2], pair_recv.at[2], partner)
    start(biases)

    @pl.when(z_lo == 1)
    def _():
        for j in range(4):
            weights[0:9, 32:64, 128 * j : 128 * j + 128] = filt[:, :, lanes(j)]

    @pl.when(gives_filters)
    def _():
        for j in range(2):
            from_partner(j).start()

    def pair_arrived(part):
        pairs[part].wait_recv()
        for direction in range(2):
            start(ring(direction, 1, part, partner_chan, own_block(part, partner_chan)))
        if part == 0:
            send_halo(partner_chan)

    def piece_wait(owner):
        slot = slot_of(owner)
        remote(packed.at[0], pieces.at[:, slot], piece_send.at[0], piece_recv.at[slot], partner).wait_recv()

    def owner_of(direction, hop):
        away = hop // 2 + 1
        base = (chan + 16 - 2 * away) % 16 if direction == 0 else (chan + 2 * away) % 16
        swap = hop % 2 == 1 if hop < 6 else direction == 1
        return base + 1 - 2 * z_lo if swap else base

    def multiply(first, slots):
        lanes_of = slice(32 * slots[0], 32 * slots[1])
        depth = 32 * (slots[1] - slots[0])
        lhs = weights[0:9, :, lanes_of].reshape(576, depth)

        def body(q, carry):
            for n in range(2):
                columns = slice(256 * n, 256 * n + 256)
                rhs = gathered[q, slots[0] : slots[1], :, columns].reshape(depth, 256)
                result = jnp.dot(lhs, rhs, preferred_element_type=F32).reshape(9, 64, 256)
                if slots[0]:
                    result = products[q, :, :, columns] + result
                products[q, :, :, columns] = result
            return carry

        lax.fori_loop(first, first + 2, body, 0)

    def multiply_halo(side):
        for slot in range(16):
            remote(give.at[0], halo.at[side, slot], halo_send.at[side, slot],
                   halo_recv.at[side, slot], twin).wait_recv()
        turned = (core + z_lo + side) % 2
        lhs = weights[pl.ds(6 * turned, 3)].reshape(192, 512)
        rhs = halo[side].reshape(512, 512)
        halo_products[side] = jnp.dot(lhs, rhs, preferred_element_type=F32).reshape(3, 64, 512)

    def block_arrived(hop, part):
        for direction in range(2):
            owner = owner_of(direction, hop)
            ring(direction, hop, part, owner, give.at[rows(part)]).wait_recv()
            onward = hop + 2 if hop < 4 or (hop == 4 and direction == 0) else None
            if hop == 5 and direction == 1:
                onward = 6
            if onward is not None:
                start(ring(direction, onward, part, owner, own_block(part, owner)))
            if part == 0:
                send_halo(owner)

    def share_pieces():
        @pl.when(z_lo == 0)
        def _():
            for m in range(2):
                owner = 2 * (x + 4 * m) + core
                piece_wait(owner)
                slot = slot_of(owner)
                for k in range(4):
                    remote(pieces.at[:, slot], pieces.at[:, slot], share_send.at[m, k],
                           piece_recv.at[slot], other_x(k) if k else twin).start()

        @pl.when(takes_filters)
        def _():
            for j in range(2):
                filters_wait(j, core)
                for k in range(3):
                    hand_on(j, k).start()

    def hand_pieces():
        @pl.when(z_lo == 0)
        def _():
            for k in range(1, 4):
                for m in range(2):
                    owner = 2 * ((x + k) % 4 + 4 * m) + core
                    piece_wait(owner)
                    slot = slot_of(owner)
                    remote(pieces.at[:, slot], pieces.at[:, slot], share_send.at[m, 3 + k],
                           piece_recv.at[slot], twin).start()

    def take_filters():
        @pl.when(z_lo == 0)
        def _():
            for k in range(4):
                for m in range(2):
                    piece_wait(2 * (k + 4 * m) + 1 - core)
            for j in range(5):
                weights[2 * j : 2 * j + 2] = pieces[j].reshape(512, 128).T.reshape(2, 64, 512)

        @pl.when(z_lo == 1)
        def _():
            for j in range(2):
                filters_wait(j, 1 - core)

            @pl.when(jnp.logical_not(inner))
            def _():
                for j in range(2):
                    filters_wait(j, core)

    pair_arrived(0)
    block_arrived(0, 0)
    pair_arrived(1)
    block_arrived(0, 1)
    block_arrived(1, 0)
    block_arrived(1, 1)
    share_pieces()
    block_arrived(2, 0)
    block_arrived(2, 1)
    block_arrived(3, 0)
    block_arrived(3, 1)
    hand_pieces()
    block_arrived(4, 0)
    block_arrived(4, 1)
    block_arrived(5, 0)
    block_arrived(5, 1)
    take_filters()
    multiply(2, (0, 8))
    block_arrived(6, 0)
    multiply(0, (0, 16))
    multiply_halo(1)

    @pl.when(outer_ok)
    def _():
        multiply_halo(0)

    @pl.when(jnp.logical_not(outer_ok))
    def _():
        halo_products[0] = jnp.zeros((3, 64, 512), F32)

    biases.wait_recv()
    block_arrived(6, 1)
    multiply(2, (8, 16))

    column = lax.broadcasted_iota(jnp.int32, (64, 512), 1)
    offset = jnp.concatenate([bias_own[:, 0:1], bias_in[:, 0:1]], axis=0)
    offset = jnp.where(z_lo == 0, offset, jnp.zeros_like(offset))

    def tap(a, b):
        return 3 * a + b + z_lo * (8 - 2 * (3 * a + b))

    def finish(r, terms, side=None):
        sums = [sum(products[q, tap(a, b)] for q, a in terms) for b in range(3)]
        if side is not None:
            sums = [s + halo_products[side, b + z_lo * (2 - 2 * b)] for b, s in enumerate(sums)]
        left, mid, right = sums
        left = jnp.where(column == 0, 0.0, pltpu.roll(left, 1, 1))
        right = jnp.where(column == 511, 0.0, pltpu.roll(right, 511, 1))
        total = (left + mid + right + offset).astype(BF16)
        low, high = total[0:32], total[32:64]
        for side, own in ((0, features), (1, image_grad)):
            @pl.when(z_lo == side)
            def _():
                own[r] = high if side else low
                staged[r] = low if side else high
                remote(staged.at[r], own.at[r], out_send.at[r], out_recv.at[r], partner).start()
        return remote(staged.at[r], features.at[r], out_send.at[r], out_recv.at[r], partner)

    outgoing = [finish(r, [(POSITION[r + a - 1], a) for a in range(3)]) for r in (1, 2)]
    outgoing.append(finish(3 - 3 * core, [(1 - core, 1), (3 - core, 2 * core)], 1))
    outgoing.append(finish(3 * core, [(core, 1), (2 + core, 2 - 2 * core)], 0))

    for copy in started:
        copy.wait_send()
    for slot in range(16):
        remote(give.at[0], halo.at[1, slot], halo_send.at[1, slot], halo_recv.at[1, slot], twin).wait_send()

    @pl.when(outer_ok)
    def _():
        for slot in range(16):
            remote(give.at[0], halo.at[0, slot], halo_send.at[0, slot], halo_recv.at[0, slot], twin).wait_send()

    @pl.when(sends_filters)
    def _():
        for d in range(1, 8):
            remote(packed.at[0], pieces.at[:, 0], piece_send.at[d], piece_recv.at[0], partner).wait_send()

        @pl.when(z_lo == 1)
        def _():
            remote(packed.at[0], pieces.at[:, 0], piece_send.at[0], piece_recv.at[0], partner).wait_send()

    @pl.when(gives_filters)
    def _():
        for j in range(2):
            from_partner(j).wait_send()

    @pl.when(z_lo == 0)
    def _():
        for m in range(2):
            for k in range(7):
                remote(pieces.at[:, 0], pieces.at[:, 0], share_send.at[m, k], piece_recv.at[0], partner).wait_send()

    @pl.when(takes_filters)
    def _():
        for j in range(2):
            for k in range(3):
                hand_on(j, k).wait_send()

    for copy in outgoing:
        copy.wait()


def per_device(image, filters, bias, upstream):
    filt = jnp.transpose(filters, (0, 2, 1))
    block = jax.ShapeDtypeStruct((4, 32, 512), BF16)
    dma = pltpu.SemaphoreType.DMA
    features, image_grad = pl.pallas_call(
        kernel,
        out_shape=(block, block),
        in_specs=[pl.BlockSpec(memory_space=pltpu.HBM)] * 4,
        out_specs=(pl.BlockSpec(memory_space=pltpu.VMEM),) * 2,
        scratch_shapes=[
            pltpu.VMEM((2, 32, 4, 512), BF16),
            pltpu.VMEM((4, 32, 512), BF16),
            pltpu.VMEM((9, 32, 512), BF16),
            pltpu.VMEM((1, 32), BF16),
            pltpu.VMEM((4, 16, 32, 512), BF16),
            pltpu.VMEM((2, 16, 32, 512), BF16),
            pltpu.VMEM((10, 64, 512), BF16),
            pltpu.VMEM((8, 5, 32, 128), BF16),
            pltpu.VMEM((5, 16, 32, 128), BF16),
            pltpu.VMEM((4, 9, 64, 512), F32),
            pltpu.VMEM((2, 3, 64, 512), F32),
            pltpu.VMEM((32, 128), F32),
            pltpu.VMEM((32, 128), F32),
            pltpu.VMEM((4, 32, 512), BF16),
            dma((4,)), dma((2, 7, 2)), dma((2, 7, 2)), dma((3,)), dma((3,)), dma((2, 16)), dma((2, 16)),
            dma((2,)), dma((4,)), dma((2, 3)), dma((8,)), dma((16,)), dma((2, 7)),
            dma((4,)), dma((4,)),
        ],
        compiler_params=pltpu.CompilerParams(
            collective_id=0, has_side_effects=True, vmem_limit_bytes=40 << 20),
        name="conv_both",
    )(*(pltpu.with_memory_space_constraint(value, pltpu.HBM)
        for value in (image, upstream, filt, bias.reshape(1, 32))))
    return tuple(jnp.transpose(value, (1, 0, 2)) for value in (features, image_grad))


def solution(mesh):
    return jax.shard_map(
        per_device,
        mesh=mesh,
        in_specs=(
            P("chan", "band", None),
            P(None, None, "chan"),
            P("chan"),
            P("chan", "band", None),
        ),
        out_specs=(P("chan", "band", None), P("chan", "band", None)),
        check_vma=False,
    )
```

time: 45.8 us -> 44.2 us (0.965)
  the two profiles are of different devices: /device:TPU:135 before, /device:TPU:151 now
where the time goes in v3:
time: 44.2 us; the launch traced here: 44 us
  Pallas kernels  41.9 us (95%)
  local copies, waits for them, and re-layouts  1.52 us (3%)
  between operations  0.64 us (1%)
    pallas_call x1, Pallas kernels, per_device(): pl.pallas_call(kernel, out_shape=(block, block), in_specs=[pl.BlockSpec(m...  41.9 us
    unnamed x2, local copies, waits for them, and re-layouts  1.52 us

profile of v3, /device:TPU:151, one launch (start us, length us, event | category | flops | bytes accessed | tf_op | source)
XLA Modules:
  0.0 44.0 jit_solution(16254332989649304754)
XLA Ops:
  0.6 41.9 %conv_both.1 = (bf16[4,32,512]{2,1,0:T(8,128)(2,1)S(1)}, bf16[4,32,512]{2,1,0:T(8,128)(2,1)S(1)}) custom-call(bf16[32,4,512]{2,1,0:T(4,128)(2,1)} %image.1, bf16[32,4,512]{2,1,0:T(4,128)(2,1)} %upstream.1, bf16[9,32,512]{2,1,0:T(8,128)(2,1)} %bitcast.6, bf16[1,32]{1,0:T(2,128)(2,1)} %bitcast.7), custom_call_target="tpu_custom_call" | custom-call | tf_op jit(solution)/shard_map/conv_both/pallas_call | solution.py:411
  42.5 0.8 %copy.6 = bf16[32,4,512]{2,1,0:T(4,128)(2,1)} copy(bf16[32,4,512]{2,0,1:T(8,128)(2,1)S(1)} %bitcast.5) | data formatting | bytes 262144
  43.3 0.8 %copy.7 = bf16[32,4,512]{2,1,0:T(4,128)(2,1)} copy(bf16[32,4,512]{2,0,1:T(8,128)(2,1)S(1)} %bitcast.4) | data formatting | bytes 262144

commit v4 on v3

--- a/solution.py
+++ b/solution.py
@@ -133,34 +133,6 @@
         for direction in range(2):
             start(ring(direction, 0, part, chan, own_block(part, chan)))
     send_halo(chan)
-    for copy in loads:
-        copy.wait()
-
-    @pl.when(sends_filters)
-    def _():
-        lane = lax.broadcasted_iota(jnp.int32, (32, 128), 1)
-        for q in range(4):
-            for j in range(5):
-                a = filt[2 * j, :, 128 * q : 128 * q + 128].astype(F32)
-                b = filt[2 * j + 1, :, 128 * q : 128 * q + 128].astype(F32) if j < 4 else a
-                packed[2 * q, j] = jnp.where(lane < 64, a, pltpu.roll(b, 64, 1)).astype(BF16)
-                packed[2 * q + 1, j] = jnp.where(lane < 64, pltpu.roll(a, 64, 1), b).astype(BF16)
-        for d in range(1, 8):
-            place = (y + d) % 8
-            slot = slot_at(chan, place)
-            remote(packed.at[place], pieces.at[:, slot], piece_send.at[d],
-                   piece_recv.at[slot], {"band": band, "chan": 2 * place}).start()
-        slot = slot_of(chan)
-
-        @pl.when(z_lo == 0)
-        def _():
-            pltpu.make_async_copy(packed.at[y], pieces.at[:, slot], piece_recv.at[slot]).start()
-
-        @pl.when(z_lo == 1)
-        def _():
-            remote(packed.at[y], pieces.at[:, slot], piece_send.at[0],
-                   piece_recv.at[slot], partner).start()
-
     turn = ((y + 7) // 2) % 4
 
     def lanes(j):
@@ -182,22 +154,52 @@
         remote(filt.at[:, :, 0:128], weights.at[0:9, 0:32, 0:128],
                relay_send.at[j, 0], filter_recv.at[2 * unit + j], twin).wait_recv()
 
-    diagonal = (lax.broadcasted_iota(jnp.int32, (32, 32), 0)
-                == lax.broadcasted_iota(jnp.int32, (32, 32), 1))
-    spread = jnp.where(diagonal, jnp.broadcast_to(bias[...].astype(F32), (32, 32)), 0.0)
-    bias_own[...] = jnp.broadcast_to(jnp.sum(spread, axis=1, keepdims=True), (32, 128))
     biases = remote(bias_own, bias_in, pair_send.at[2], pair_recv.at[2], partner)
-    start(biases)
-
-    @pl.when(z_lo == 1)
-    def _():
-        for j in range(4):
-            weights[0:9, 32:64, 128 * j : 128 * j + 128] = filt[:, :, lanes(j)]
-
-    @pl.when(gives_filters)
-    def _():
-        for j in range(2):
-            from_partner(j).start()
+
+    def prepare():
+        for copy in loads:
+            copy.wait()
+
+        @pl.when(sends_filters)
+        def _():
+            lane = lax.broadcasted_iota(jnp.int32, (32, 128), 1)
+            for q in range(4):
+                for j in range(5):
+                    a = filt[2 * j, :, 128 * q : 128 * q + 128].astype(F32)
+                    b = filt[2 * j + 1, :, 128 * q : 128 * q + 128].astype(F32) if j < 4 else a
+                    packed[2 * q, j] = jnp.where(lane < 64, a, pltpu.roll(b, 64, 1)).astype(BF16)
+                    packed[2 * q + 1, j] = jnp.where(lane < 64, pltpu.roll(a, 64, 1), b).astype(BF16)
+            for d in range(1, 8):
+                place = (y + d) % 8
+                slot = slot_at(chan, place)
+                remote(packed.at[place], pieces.at[:, slot], piece_send.at[d],
+                       piece_recv.at[slot], {"band": band, "chan": 2 * place}).start()
+            slot = slot_of(chan)
+
+            @pl.when(z_lo == 0)
+            def _():
+                pltpu.make_async_copy(packed.at[y], pieces.at[:, slot], piece_recv.at[slot]).start()
+
+            @pl.when(z_lo == 1)
+            def _():
+                remote(packed.at[y], pieces.at[:, slot], piece_send.at[0],
+                       piece_recv.at[slot], partner).start()
+
+        diagonal = (lax.broadcasted_iota(jnp.int32, (32, 32), 0)
+                    == lax.broadcasted_iota(jnp.int32, (32, 32), 1))
+        spread = jnp.where(diagonal, jnp.broadcast_to(bias[...].astype(F32), (32, 32)), 0.0)
+        bias_own[...] = jnp.broadcast_to(jnp.sum(spread, axis=1, keepdims=True), (32, 128))
+        start(biases)
+
+        @pl.when(z_lo == 1)
+        def _():
+            for j in range(4):
+                weights[0:9, 32:64, 128 * j : 128 * j + 128] = filt[:, :, lanes(j)]
+
+        @pl.when(gives_filters)
+        def _():
+            for j in range(2):
+                from_partner(j).start()
 
     def pair_arrived(part):
         pairs[part].wait_recv()
@@ -302,36 +304,28 @@
                 for j in range(2):
                     filters_wait(j, core)
 
+    prepare()
     pair_arrived(0)
     block_arrived(0, 0)
     pair_arrived(1)
+    block_arrived(1, 0)
     block_arrived(0, 1)
-    block_arrived(1, 0)
+    block_arrived(2, 0)
     block_arrived(1, 1)
     share_pieces()
-    block_arrived(2, 0)
+    block_arrived(3, 0)
     block_arrived(2, 1)
-    block_arrived(3, 0)
+    block_arrived(4, 0)
     block_arrived(3, 1)
     hand_pieces()
-    block_arrived(4, 0)
+    block_arrived(5, 0)
     block_arrived(4, 1)
-    block_arrived(5, 0)
+    block_arrived(6, 0)
     block_arrived(5, 1)
     take_filters()
     multiply(2, (0, 8))
-    block_arrived(6, 0)
     multiply(0, (0, 16))
     multiply_halo(1)
-
-    @pl.when(outer_ok)
-    def _():
-        multiply_halo(0)
-
-    @pl.when(jnp.logical_not(outer_ok))
-    def _():
-        halo_products[0] = jnp.zeros((3, 64, 512), F32)
-
     biases.wait_recv()
     block_arrived(6, 1)
     multiply(2, (8, 16))
@@ -362,6 +356,15 @@
 
     outgoing = [finish(r, [(POSITION[r + a - 1], a) for a in range(3)]) for r in (1, 2)]
     outgoing.append(finish(3 - 3 * core, [(1 - core, 1), (3 - core, 2 * core)], 1))
+
+    @pl.when(outer_ok)
+    def _():
+        multiply_halo(0)
+
+    @pl.when(jnp.logical_not(outer_ok))
+    def _():
+        halo_products[0] = jnp.zeros((3, 64, 512), F32)
+
     outgoing.append(finish(3 * core, [(core, 1), (2 + core, 2 - 2 * core)], 0))
 
     for copy in started:

time: 44.2 us -> 41.6 us (0.941)
  the two profiles are of different devices: /device:TPU:151 before, /device:TPU:72 now
where the time goes in v4:
time: 41.6 us; the launch traced here: 41.5 us
  Pallas kernels  39.3 us (94%)
  local copies, waits for them, and re-layouts  1.52 us (4%)
  between operations  0.64 us (2%)
    pallas_call x1, Pallas kernels, per_device(): pl.pallas_call(kernel, out_shape=(block, block), in_specs=[pl.BlockSpec(m...  39.3 us
    unnamed x2, local copies, waits for them, and re-layouts  1.52 us

profile of v4, /device:TPU:72, one launch (start us, length us, event | category | flops | bytes accessed | tf_op | source)
XLA Modules:
  0.0 41.5 jit_solution(4287498938359046415)
XLA Ops:
  0.6 39.3 %conv_both.1 = (bf16[4,32,512]{2,1,0:T(8,128)(2,1)S(1)}, bf16[4,32,512]{2,1,0:T(8,128)(2,1)S(1)}) custom-call(bf16[32,4,512]{2,1,0:T(4,128)(2,1)} %image.1, bf16[32,4,512]{2,1,0:T(4,128)(2,1)} %upstream.1, bf16[9,32,512]{2,1,0:T(8,128)(2,1)} %bitcast.6, bf16[1,32]{1,0:T(2,128)(2,1)} %bitcast.7), custom_call_target="tpu_custom_call" | custom-call | tf_op jit(solution)/shard_map/conv_both/pallas_call | solution.py:414
  39.9 0.8 %copy.6 = bf16[32,4,512]{2,1,0:T(4,128)(2,1)} copy(bf16[32,4,512]{2,0,1:T(8,128)(2,1)S(1)} %bitcast.5) | data formatting | bytes 262144
  40.7 0.8 %copy.7 = bf16[32,4,512]{2,1,0:T(4,128)(2,1)} copy(bf16[32,4,512]{2,0,1:T(8,128)(2,1)S(1)} %bitcast.4) | data formatting | bytes 262144

commit v5 on v4

--- a/solution.py
+++ b/solution.py
@@ -312,13 +312,13 @@
     block_arrived(0, 1)
     block_arrived(2, 0)
     block_arrived(1, 1)
+    block_arrived(3, 0)
     share_pieces()
-    block_arrived(3, 0)
     block_arrived(2, 1)
     block_arrived(4, 0)
     block_arrived(3, 1)
+    block_arrived(5, 0)
     hand_pieces()
-    block_arrived(5, 0)
     block_arrived(4, 1)
     block_arrived(6, 0)
     block_arrived(5, 1)
@@ -404,6 +404,16 @@
                 hand_on(j, k).wait_send()
 
     for copy in outgoing:
+        copy.wait()
+
+
+def channels_first(features, image_grad, features_out, image_grad_out, turned, sem):
+    copies = []
+    for k, (source, out) in enumerate(((features, features_out), (image_grad, image_grad_out))):
+        turned[k] = jnp.transpose(source[...], (1, 0, 2))
+        copies.append(pltpu.make_async_copy(turned.at[k], out, sem.at[k]))
+        copies[-1].start()
+    for copy in copies:
         copy.wait()
 
 
@@ -440,7 +450,16 @@
         name="conv_both",
     )(*(pltpu.with_memory_space_constraint(value, pltpu.HBM)
         for value in (image, upstream, filt, bias.reshape(1, 32))))
-    return tuple(jnp.transpose(value, (1, 0, 2)) for value in (features, image_grad))
+    result = jax.ShapeDtypeStruct((32, 4, 512), BF16)
+    return pl.pallas_call(
+        channels_first,
+        out_shape=(result, result),
+        in_specs=[pl.BlockSpec(memory_space=pltpu.VMEM)] * 2,
+        out_specs=(pl.BlockSpec(memory_space=pltpu.HBM),) * 2,
+        scratch_shapes=[pltpu.VMEM((2, 32, 4, 512), BF16), dma((2,))],
+        compiler_params=pltpu.CompilerParams(vmem_limit_bytes=8 << 20),
+        name="channels_first",
+    )(features, image_grad)
 
 
 def solution(mesh):

time: 41.6 us -> 40.7 us (0.978)
  the two profiles are of different devices: /device:TPU:72 before, /device:TPU:8 now
where the time goes in v5:
time: 40.7 us; the launch traced here: 40.6 us
  Pallas kernels  39.9 us (98%)
  between operations  0.64 us (2%)
    pallas_call x1, Pallas kernels, per_device(): pl.pallas_call(kernel, out_shape=(block, block), in_specs=[pl.BlockSpec(m...  39.2 us

profile of v5, /device:TPU:8, one launch (start us, length us, event | category | flops | bytes accessed | tf_op | source)
XLA Modules:
  0.0 40.6 jit_solution(1066411262902088378)
XLA Ops:
  0.6 39.2 %conv_both.1 = (bf16[4,32,512]{2,1,0:T(8,128)(2,1)S(1)}, bf16[4,32,512]{2,1,0:T(8,128)(2,1)S(1)}) custom-call(bf16[32,4,512]{2,1,0:T(4,128)(2,1)} %image.1, bf16[32,4,512]{2,1,0:T(4,128)(2,1)} %upstream.1, bf16[9,32,512]{2,1,0:T(8,128)(2,1)} %bitcast.2, bf16[1,32]{1,0:T(2,128)(2,1)} %bitcast.3), custom_call_target="tpu_custom_call" | custom-call | tf_op jit(solution)/shard_map/conv_both/pallas_call | solution.py:424
  39.8 0.7 %channels_first.1 = (bf16[32,4,512]{2,1,0:T(4,128)(2,1)}, bf16[32,4,512]{2,1,0:T(4,128)(2,1)}) custom-call(bf16[4,32,512]{2,1,0:T(8,128)(2,1)S(1)} %get-tuple-element.4.features, bf16[4,32,512]{2,1,0:T(8,128)(2,1)S(1)} %get-tuple-element.5.image_grad), custom_call_target="tpu_custom_call" | custom-call | tf_op jit(solution)/shard_map/channels_first/pallas_call | solution.py:454

commit v6 on v5

--- a/solution.py
+++ b/solution.py
@@ -67,7 +67,7 @@
     def _():
         greet(outer)
 
-    @pl.when(z_lo == 0)
+    @pl.when(z_lo == core)
     def _():
         for m in range(2):
             source = 2 * (x + 4 * m) + core
@@ -75,6 +75,9 @@
             @pl.when(source != chan)
             def _():
                 greet({"band": band, "chan": source})
+
+    @pl.when(z_lo == 0)
+    def _():
         for k in range(1, 4):
             greet(other_x(k))
 
@@ -91,7 +94,7 @@
         give[POSITION[row]] = natural[1, :, row, :]
 
     targets = 4 + jnp.where(outer_ok, 1, 0) + jnp.where(z_lo == 0, 3, 0)
-    targets = targets + jnp.where(sends_filters, 7 + z_lo, 0) + jnp.where(takes_filters, 2, 0)
+    targets = targets + jnp.where(sends_filters, 7, 0) + jnp.where(takes_filters, 2, 0)
     pl.semaphore_wait(barrier, targets)
 
     def rows(part):
@@ -173,7 +176,7 @@
                 place = (y + d) % 8
                 slot = slot_at(chan, place)
                 remote(packed.at[place], pieces.at[:, slot], piece_send.at[d],
-                       piece_recv.at[slot], {"band": band, "chan": 2 * place}).start()
+                       piece_recv.at[slot], {"band": band, "chan": 2 * place + z_lo}).start()
             slot = slot_of(chan)
 
             @pl.when(z_lo == 0)
@@ -256,6 +259,26 @@
             if part == 0:
                 send_halo(owner)
 
+    def cross(m):
+        owner = 2 * (x + 4 * m) + core
+        slot = slot_of(owner)
+        return owner, remote(pieces.at[:, slot], pieces.at[:, slot], share_send.at[m, 0],
+                             piece_recv.at[slot], partner)
+
+    def cross_pieces(ending):
+        @pl.when((z_lo == 1) & (core == 1))
+        def _():
+            for m in range(2):
+                owner, copy = cross(m)
+
+                @pl.when(owner != chan)
+                def _():
+                    if ending:
+                        copy.wait_send()
+                    else:
+                        piece_wait(owner)
+                        copy.start()
+
     def share_pieces():
         @pl.when(z_lo == 0)
         def _():
@@ -310,6 +333,7 @@
     pair_arrived(1)
     block_arrived(1, 0)
     block_arrived(0, 1)
+    cross_pieces(False)
     block_arrived(2, 0)
     block_arrived(1, 1)
     block_arrived(3, 0)
@@ -376,6 +400,8 @@
     def _():
         for slot in range(16):
             remote(give.at[0], halo.at[0, slot], halo_send.at[0, slot], halo_recv.at[0, slot], twin).wait_send()
+
+    cross_pieces(True)
 
     @pl.when(sends_filters)
     def _():

time: 40.7 us -> 40.6 us (level)
  the two profiles are of different devices: /device:TPU:8 before, /device:TPU:88 now
where the time goes in v6:
time: 40.6 us; the launch traced here: 40.5 us
  Pallas kernels  39.8 us (98%)
  between operations  0.64 us (2%)
    pallas_call x1, Pallas kernels, per_device(): pl.pallas_call(kernel, out_shape=(block, block), in_specs=[pl.BlockSpec(m...  39.1 us

profile of v6, /device:TPU:88, one launch (start us, length us, event | category | flops | bytes accessed | tf_op | source)
XLA Modules:
  0.0 40.5 jit_solution(9014962352845239764)
XLA Ops:
  0.6 39.1 %conv_both.1 = (bf16[4,32,512]{2,1,0:T(8,128)(2,1)S(1)}, bf16[4,32,512]{2,1,0:T(8,128)(2,1)S(1)}) custom-call(bf16[32,4,512]{2,1,0:T(4,128)(2,1)} %image.1, bf16[32,4,512]{2,1,0:T(4,128)(2,1)} %upstream.1, bf16[9,32,512]{2,1,0:T(8,128)(2,1)} %bitcast.2, bf16[1,32]{1,0:T(2,128)(2,1)} %bitcast.3), custom_call_target="tpu_custom_call" | custom-call | tf_op jit(solution)/shard_map/conv_both/pallas_call | solution.py:450
  39.7 0.7 %channels_first.1 = (bf16[32,4,512]{2,1,0:T(4,128)(2,1)}, bf16[32,4,512]{2,1,0:T(4,128)(2,1)}) custom-call(bf16[4,32,512]{2,1,0:T(8,128)(2,1)S(1)} %get-tuple-element.4.features, bf16[4,32,512]{2,1,0:T(8,128)(2,1)S(1)} %get-tuple-element.5.image_grad), custom_call_target="tpu_custom_call" | custom-call | tf_op jit(solution)/shard_map/channels_first/pallas_call | solution.py:480

commit v7 on v6

--- a/solution.py
+++ b/solution.py
@@ -43,25 +43,25 @@
              pltpu.make_async_copy(bias_row, bias, load_sem.at[3])]
     keeping = [pltpu.make_async_copy(image, natural.at[z_lo], load_sem.at[0]),
                pltpu.make_async_copy(upstream, natural.at[1 - z_lo], load_sem.at[1])]
+    barrier = pltpu.get_barrier_semaphore()
+
+    def greet(where):
+        pl.semaphore_signal(barrier, inc=1, device_id=where, device_id_type=MESH)
+
+    def other_x(k):
+        return {"band": z_hi * 8 + ((x + k) % 4) * 2 + core, "chan": chan}
+
+    inner = (x == 1) | (x == 2)
+    gives_filters, takes_filters = (z_lo == 0) & inner, (z_lo == 1) & inner
+
+    def at_x(place, unit):
+        return {"band": z_hi * 8 + place * 2 + unit, "chan": chan}
+
+    for where in (*ring_next, partner):
+        greet(where)
     for copy in keeping + loads:
         copy.start()
-
-    barrier = pltpu.get_barrier_semaphore()
-
-    def greet(where):
-        pl.semaphore_signal(barrier, inc=1, device_id=where, device_id_type=MESH)
-
-    def other_x(k):
-        return {"band": z_hi * 8 + ((x + k) % 4) * 2 + core, "chan": chan}
-
-    inner = (x == 1) | (x == 2)
-    gives_filters, takes_filters = (z_lo == 0) & inner, (z_lo == 1) & inner
-
-    def at_x(place, unit):
-        return {"band": z_hi * 8 + place * 2 + unit, "chan": chan}
-
-    for where in (partner, *ring_next, twin):
-        greet(where)
+    greet(twin)
 
     @pl.when(outer_ok)
     def _():
@@ -238,14 +238,18 @@
 
         lax.fori_loop(first, first + 2, body, 0)
 
-    def multiply_halo(side):
-        for slot in range(16):
+    def multiply_halo(side, slots=(0, 16)):
+        for slot in range(*slots):
             remote(give.at[0], halo.at[side, slot], halo_send.at[side, slot],
                    halo_recv.at[side, slot], twin).wait_recv()
         turned = (core + z_lo + side) % 2
-        lhs = weights[pl.ds(6 * turned, 3)].reshape(192, 512)
-        rhs = halo[side].reshape(512, 512)
-        halo_products[side] = jnp.dot(lhs, rhs, preferred_element_type=F32).reshape(3, 64, 512)
+        depth = 32 * (slots[1] - slots[0])
+        lhs = weights[pl.ds(6 * turned, 3), :, 32 * slots[0] : 32 * slots[1]].reshape(192, depth)
+        rhs = halo[side, slots[0] : slots[1]].reshape(depth, 512)
+        result = jnp.dot(lhs, rhs, preferred_element_type=F32).reshape(3, 64, 512)
+        if slots[0]:
+            result = halo_products[side] + result
+        halo_products[side] = result
 
     def block_arrived(hop, part):
         for direction in range(2):
@@ -350,6 +354,15 @@
     multiply(2, (0, 8))
     multiply(0, (0, 16))
     multiply_halo(1)
+
+    @pl.when(outer_ok)
+    def _():
+        multiply_halo(0, (0, 8))
+
+    @pl.when(jnp.logical_not(outer_ok))
+    def _():
+        halo_products[0] = jnp.zeros((3, 64, 512), F32)
+
     biases.wait_recv()
     block_arrived(6, 1)
     multiply(2, (8, 16))
@@ -383,11 +396,7 @@
 
     @pl.when(outer_ok)
     def _():
-        multiply_halo(0)
-
-    @pl.when(jnp.logical_not(outer_ok))
-    def _():
-        halo_products[0] = jnp.zeros((3, 64, 512), F32)
+        multiply_halo(0, (8, 16))
 
     outgoing.append(finish(3 * core, [(core, 1), (2 + core, 2 - 2 * core)], 0))
 

time: 40.6 us -> 40.6 us (level)
  no operation moved by 1% of the time
where the time goes in v7:
time: 40.6 us; the launch traced here: 40.4 us
  Pallas kernels  39.8 us (98%)
  between operations  0.64 us (2%)
    pallas_call x1, Pallas kernels, per_device(): pl.pallas_call(kernel, out_shape=(block, block), in_specs=[pl.BlockSpec(m...  39.1 us

profile of v7, /device:TPU:88, one launch (start us, length us, event | category | flops | bytes accessed | tf_op | source)
XLA Modules:
  0.0 40.4 jit_solution(11367413701315457624)
XLA Ops:
  0.6 39.1 %conv_both.1 = (bf16[4,32,512]{2,1,0:T(8,128)(2,1)S(1)}, bf16[4,32,512]{2,1,0:T(8,128)(2,1)S(1)}) custom-call(bf16[32,4,512]{2,1,0:T(4,128)(2,1)} %image.1, bf16[32,4,512]{2,1,0:T(4,128)(2,1)} %upstream.1, bf16[9,32,512]{2,1,0:T(8,128)(2,1)} %bitcast.2, bf16[1,32]{1,0:T(2,128)(2,1)} %bitcast.3), custom_call_target="tpu_custom_call" | custom-call | tf_op jit(solution)/shard_map/conv_both/pallas_call | solution.py:459
  39.7 0.7 %channels_first.1 = (bf16[32,4,512]{2,1,0:T(4,128)(2,1)}, bf16[32,4,512]{2,1,0:T(4,128)(2,1)}) custom-call(bf16[4,32,512]{2,1,0:T(8,128)(2,1)S(1)} %get-tuple-element.4.features, bf16[4,32,512]{2,1,0:T(8,128)(2,1)S(1)} %get-tuple-element.5.image_grad), custom_call_target="tpu_custom_call" | custom-call | tf_op jit(solution)/shard_map/channels_first/pallas_call | solution.py:489
